TPU v7x, 512 devices: a whole 4x8x8 slice. The times are simulated.
512 devices in a mesh: dp: 64 (over y, x, core), tensor: 8 (over z).
Axes of the slice: x: 4, y: 8, z: 8, core: 2. Of those that a mesh axis runs over, the one named last changes fastest.
Arguments:
- hidden_act: bfloat16 [32768, 1408], P('dp', 'tensor'), may hold values from -6 to 6
- cotangent: bfloat16 [32768, 2048], P('dp', 'tensor'), may hold values from -4 to 4
- down_table: bfloat16 [1408, 64, 2048], P('tensor', 'dp'), may hold values from -0.15625 to 0.15625
- expert_ids: int32 [128, 4], P('dp'), may hold values from 0 to 31, as said below
- merge_weights: float32 [128, 4], P('dp'), may hold values from 0.1 to 1
- owner_slot: int32 [32], replicated, may hold values from 0 to 63, as said below
Outputs:
- layer_out: bfloat16 [32768, 2048], P('dp', 'tensor')
- grad_hidden: bfloat16 [32768, 1408], P('dp', 'tensor')
- expert_grad: float32 [1408, 64, 2048], P('tensor', 'dp')
Inputs may be any that keep to these rules, and one draw needn't show every extreme that they name: `expert_ids`: each segment lists 4 different experts; the 2 segments of one index of dp list exactly 6 different experts together. `owner_slot`: different experts have different slots; slot 63 always holds an expert.
All inputs are finite; a program needn't handle non-finite values.
Results may differ from a plain program's by a relative error of at most 0.013.
Values may be sent and summed in bfloat16 or wider, within the bound.
A program may use at most 128 MiB of HBM per device.

v0:
```python
import jax
import jax.numpy as jnp
from jax import lax
from jax.sharding import PartitionSpec as P

E = 32
K = 4
POOL = 6


def pool_members(id_rows):
    listed = id_rows.reshape(-1)
    experts = jnp.arange(E, dtype=jnp.int32)
    present = jnp.any(listed[None, :] == experts[:, None], axis=1)
    ranking = jnp.cumsum(present.astype(jnp.int32)) - 1
    places = jnp.arange(POOL, dtype=jnp.int32)
    chosen = present[None, :] & (ranking[None, :] == places[:, None])
    return jnp.sum(jnp.where(chosen, experts[None, :], 0), axis=1)


def merge_coefficients(id_rows, weight_rows, targets):
    matches = id_rows[:, :, None] == targets[None, None, :]
    return jnp.sum(jnp.where(matches, weight_rows[:, :, None], 0.0), axis=1)


def body(hidden_act, cotangent, down_table, expert_ids, merge_weights, owner_slot):
    dp_count = lax.axis_size("dp")
    seg_count = expert_ids.shape[0]
    ff_local, slot_local, width = down_table.shape
    stripe = width // dp_count
    row_count = hidden_act.shape[0]
    seg_len = row_count // seg_count
    every_expert = jnp.arange(E, dtype=jnp.int32)
    all_ids, all_weights = (
        lax.all_gather(expert_ids, "dp", axis=0, tiled=True),
        lax.all_gather(merge_weights, "dp", axis=0, tiled=True),
    )
    ids_by_dev = all_ids.reshape(dp_count, seg_count, K)
    weights_by_dev = all_weights.reshape(dp_count, seg_count, K)
    pools_all = jax.vmap(pool_members)(ids_by_dev)
    my_pool = pools_all[lax.axis_index("dp")]
    my_coef = merge_coefficients(expert_ids, merge_weights, my_pool)
    member_table = (pools_all.T[:, :, None] == every_expert[None, None, :]).astype(jnp.bfloat16)
    stripes = lax.all_to_all(down_table, "dp", split_axis=2, concat_axis=1, tiled=True)
    by_expert = jnp.take(stripes, owner_slot, axis=1)
    outgoing = jnp.take(by_expert, pools_all.T, axis=1).reshape(ff_local, POOL, width)
    panel_set = lax.all_to_all(outgoing, "dp", split_axis=2, concat_axis=2, tiled=True)
    merged = jnp.sum(
        panel_set[:, None, :, :].astype(jnp.float32) * my_coef[None, :, :, None], axis=2
    ).astype(jnp.bfloat16)
    hidden_seg = hidden_act.reshape(seg_count, seg_len, ff_local)
    partial_rows = jnp.einsum(
        "stf,fsd->std", hidden_seg, merged, preferred_element_type=jnp.float32
    ).reshape(row_count, width)
    layer_out = lax.psum_scatter(
        partial_rows.astype(jnp.bfloat16), "tensor", scatter_dimension=1, tiled=True
    )
    full_cot = lax.all_gather(cotangent, "tensor", axis=1, tiled=True)
    cot_seg = full_cot.reshape(seg_count, seg_len, width)
    grad_hidden = (
        jnp.einsum("std,fsd->stf", cot_seg, merged, preferred_element_type=jnp.float32)
        .astype(jnp.bfloat16)
        .reshape(row_count, ff_local)
    )
    seg_grads = jnp.einsum(
        "stf,std->fsd", hidden_seg, cot_seg, preferred_element_type=jnp.float32
    ).astype(jnp.bfloat16)
    returned = lax.all_to_all(seg_grads, "dp", split_axis=2, concat_axis=2, tiled=True).reshape(
        ff_local, seg_count, dp_count, stripe
    )
    pool_coef = jax.vmap(merge_coefficients)(ids_by_dev, weights_by_dev, pools_all)
    coef_view = jnp.transpose(pool_coef, (1, 2, 0))
    group_sums = jnp.sum(
        returned[:, :, None, :, :].astype(jnp.float32) * coef_view[None, :, :, :, None], axis=1
    ).astype(jnp.bfloat16)
    grad_stripes = jnp.einsum(
        "fprd,pre->fed", group_sums, member_table, preferred_element_type=jnp.float32
    )
    slotted = (
        jnp.zeros((ff_local, slot_local * dp_count, stripe), jnp.float32)
        .at[:, owner_slot, :]
        .set(grad_stripes)
    )
    expert_grad = lax.all_to_all(
        slotted.astype(jnp.bfloat16), "dp", split_axis=1, concat_axis=2, tiled=True
    ).astype(slotted.dtype)
    return (layer_out, grad_hidden, expert_grad)


def solution(mesh):
    placed = (
        P("dp", "tensor"),
        P("dp", "tensor"),
        P("tensor", "dp", None),
        P("dp", None),
        P("dp", None),
        P(),
    )
    return jax.shard_map(
        body,
        mesh=mesh,
        in_specs=placed,
        out_specs=(P("dp", "tensor"), P("dp", "tensor"), P("tensor", "dp", None)),
        check_vma=False,
    )
```

profile of v0, /device:TPU:1, one launch (start us, length us, event | category | flops | bytes accessed | tf_op | source)
XLA Modules:
  0.0 478.6 jit_solution(9711148216334973201)
XLA Ops:
  7.2 4.5 copy.81
  12.2 11.6 %reduce.2 = bf16[2048,176]{1,0:T(8,128)(2,1)S(1)} reduce(bf16[2048,1,176]{2,1,0:T(2,128)(2,1)S(1)} %bitcast.55, bf16[]{:T(256)} %broadcast.42), dimensions={1}, to_apply=%bitcast.44.reduce_sub_computation | reduce | bytes 1441794
  23.9 2.6 reshape.124
  26.5 11.6 %all-to-all-start = ((bf16[64,2,2816]{2,1,0:T(2,128)(2,1)}), bf16[64,2,2816]{2,1,0:T(2,128)(2,1)S(1)}, u32[]{:S(2)}, u32[]{:S(2)}) async-start(bf16[64,2,2816]{2,1,0:T(2,128)(2,1)} %reshape.124), calls=%async_computation | async-start | bytes 1441792 | tf_op jit(solution)/shard_map/all_to_all | solution.py:44
  38.1 50.6 %all-gather = s32[64,2,4]{2,1,0:T(2,128)S(1)} all-gather(s32[1,2,4]{2,1,0:T(2,128)S(1)} %bitcast.65), channel_id=1, replica_groups=mesh['dp'=64,'tensor'=8] {'dp'}, dimensions={0}, use_global_device_ids=true | all-gather | bytes 2080 | tf_op jit(solution)/shard_map/all_gather | solution.py:35
  89.8 3.2 reshape.125
  93.8 13.3 %gather_fusion.1 = bf16[384,176,32]{1,2,0:T(8,128)(2,1)} fusion(bf16[176,32,32]{0,2,1:T(8,128)(2,1)S(1)} %select_bitcast_fusion, s32[1024]{0:T(1024)S(1)} %pad_clamp_fusion), kind=kCustom, calls=%fused_computation.1 | custom fusion | bytes 8652288 | tf_op jit(solution)/shard_map/jit(_take)/gather | solution.py:46
  107.2 6.2 %broadcast_select_fusion = bf16[176,6,2048]{0,2,1:T(8,128)(2,1)S(1)} fusion(bf16[176,6,2048]{0,2,1:T(8,128)(2,1)} %bitcast.51, pred[6,2048]{1,0:T(8,128)(4,1)S(1)} %broadcast_in_dim.86), kind=kLoop, calls=%fused_computation.7 | loop fusion | flops 2162688 | bytes 8663040 | tf_op jit(solution)/shard_map/jit(_take)/select_n | solution.py:46
  113.4 22.3 %copy.82 = bf16[176,6,2048]{0,1,2:T(8,128)(2,1)} copy(bf16[176,6,2048]{0,2,1:T(8,128)(2,1)S(1)} %broadcast_select_fusion) | data formatting | bytes 8650752 | tf_op jit(solution)/shard_map/jit(_take)/select_n | solution.py:46
  135.7 8.6 %all-to-all-start.1 = ((bf16[176,6,2048]{0,1,2:T(8,128)(2,1)}), bf16[176,6,2048]{0,1,2:T(8,128)(2,1)}, u32[]{:S(2)}, u32[]{:S(2)}) async-start(bf16[176,6,2048]{0,1,2:T(8,128)(2,1)} %copy.82), calls=%async_computation.1 | async-start | bytes 16777216 | tf_op jit(solution)/shard_map/all_to_all | solution.py:47
  145.1 53.0 %all-gather.4.cloned.1.call-done = bf16[512,2048]{1,0:T(8,128)(2,1)} async-done(((bf16[512,256]{1,0:T(8,128)(2,1)}), bf16[512,2048]{1,0:T(8,128)(2,1)}) %all-gather.4.cloned.1.call-update) | async-done | bytes 2097168 | tf_op jit(solution)/shard_map/all_gather | solution.py:58
  198.0 2.1 fusion.2
  200.2 3.8 copy.87
  204.0 122.7 %all-to-all-done.1 = bf16[176,6,2048]{0,1,2:T(8,128)(2,1)} async-done(((bf16[176,6,2048]{0,1,2:T(8,128)(2,1)}), bf16[176,6,2048]{0,1,2:T(8,128)(2,1)}, u32[]{:S(2)}, u32[]{:S(2)}) %all-to-all-start.1) | async-done | bytes 4325408 | tf_op jit(solution)/shard_map/all_to_all | solution.py:47
  326.7 10.1 %all-to-all-start.2 = ((bf16[176,2,2048]{0,1,2:T(2,128)(2,1)}), bf16[176,2,2048]{0,1,2:T(2,128)(2,1)S(1)}, u32[]{:S(2)}, u32[]{:S(2)}) async-start(bf16[176,2,2048]{0,1,2:T(2,128)(2,1)} %copy.87), calls=%async_computation.3 | async-start | bytes 4194304 | tf_op jit(solution)/shard_map/all_to_all | solution.py:68
  337.1 11.3 %copy.83 = bf16[176,6,2048]{2,0,1:T(8,128)(2,1)} copy(bf16[176,6,2048]{0,1,2:T(8,128)(2,1)} %all-to-all-done.1) | data formatting | bytes 8650752 | tf_op jit(solution)/shard_map/all_to_all | solution.py:47
  348.4 6.6 %convert_element_type.68 = f32[176,6,2048]{2,0,1:T(8,128)} convert(bf16[176,6,2048]{2,0,1:T(8,128)(2,1)} %copy.83) | non-fusion elementwise | flops 2162688 | bytes 12976128 | tf_op jit(solution)/shard_map/convert_element_type | solution.py:49
  355.0 4.8 multiply_reduce_fusion.1
  360.9 2.1 convolution_convert_fusion
  363.0 53.9 %all-gather.1 = f32[64,2,4]{2,1,0:T(2,128)S(1)} all-gather(f32[1,2,4]{2,1,0:T(2,128)S(1)} %bitcast.66), channel_id=1, replica_groups=mesh['dp'=64,'tensor'=8] {'dp'}, dimensions={0}, use_global_device_ids=true | all-gather | bytes 2080 | tf_op jit(solution)/shard_map/all_gather | solution.py:36
  417.7 4.2 multiply_reduce_fusion
  421.9 3.7 fusion.3
  428.2 35.5 %all_to_all.31 = bf16[176,64,32]{0,2,1:T(8,128)(2,1)S(1)} all-to-all(bf16[176,64,32]{0,2,1:T(8,128)(2,1)S(1)} %convert_element_type.80), channel_id=1, replica_groups=mesh['dp'=64,'tensor'=8] {'dp'}, dimensions={1} | all-to-all | bytes 1441792 | tf_op jit(solution)/shard_map/all_to_all | solution.py:84
  465.2 5.1 %copy.93 = f32[176,1,2048]{2,1,0:T(1,128)} copy(f32[176,1,2048]{0,2,1:T(8,128)} %bitcast_convert_fusion) | data formatting | bytes 2883584
  (54 shorter events, 10.8 us)
Async XLA Ops:
  23.9 14.3 %copy-start.4 = (s32[2,4]{1,0:T(2,128)S(1)}, s32[2,4]{1,0:T(2,128)}, u32[]{:S(2)}) copy-start(s32[2,4]{1,0:T(2,128)} %param.9) | copy-start | bytes 100
  23.9 65.9 %copy-start.6 = (s32[32]{0:T(128)S(1)}, s32[32]{0:T(128)}, u32[]{:S(2)}) copy-start(s32[32]{0:T(128)} %param.11) | copy-start | bytes 388
  26.5 63.3 %all-to-all-start = ((bf16[64,2,2816]{2,1,0:T(2,128)(2,1)}), bf16[64,2,2816]{2,1,0:T(2,128)(2,1)S(1)}, u32[]{:S(2)}, u32[]{:S(2)}) async-start(bf16[64,2,2816]{2,1,0:T(2,128)(2,1)} %reshape.124), calls=%async_computation | async-start | bytes 1441792 | tf_op jit(solution)/shard_map/all_to_all | solution.py:44
  135.7 62.3 %copy-start.3 = (bf16[512,176]{0,1:T(8,128)(2,1)S(1)}, bf16[512,176]{0,1:T(8,128)(2,1)}, u32[]{:S(2)}) copy-start(bf16[512,176]{0,1:T(8,128)(2,1)} %param.6) | copy-start | bytes 540676
  135.7 191.0 %all-to-all-start.1 = ((bf16[176,6,2048]{0,1,2:T(8,128)(2,1)}), bf16[176,6,2048]{0,1,2:T(8,128)(2,1)}, u32[]{:S(2)}, u32[]{:S(2)}) async-start(bf16[176,6,2048]{0,1,2:T(8,128)(2,1)} %copy.82), calls=%async_computation.1 | async-start | bytes 16777216 | tf_op jit(solution)/shard_map/all_to_all | solution.py:47
  144.3 53.7 %all-gather.4.cloned.1.call-start = ((), (), s32[]{:S(2)}) async-start(), calls=%async_computation.6 | async-start | bytes 2359296 | tf_op jit(solution)/shard_map/all_gather | solution.py:58
  204.0 133.0 %copy-start.5 = (f32[2,4]{1,0:T(2,128)S(1)}, f32[2,4]{1,0:T(2,128)}, u32[]{:S(2)}) copy-start(f32[2,4]{1,0:T(2,128)} %param.10) | copy-start | bytes 100
  326.7 90.3 %all-to-all-start.2 = ((bf16[176,2,2048]{0,1,2:T(2,128)(2,1)}), bf16[176,2,2048]{0,1,2:T(2,128)(2,1)S(1)}, u32[]{:S(2)}, u32[]{:S(2)}) async-start(bf16[176,2,2048]{0,1,2:T(2,128)(2,1)} %copy.87), calls=%async_computation.3 | async-start | bytes 4194304 | tf_op jit(solution)/shard_map/all_to_all | solution.py:68
  336.8 135.0 %reduce-scatter.2.cloned.1.call-start = ((), (), s32[]{:S(2)}) async-start(), calls=%async_computation.5 | async-start | bytes 2359296 | tf_op jit(solution)/shard_map/reduce_scatter | solution.py:55
  359.8 1.1 copy-start
  465.2 5.1 %copy-start.1 = (bf16[176,2,2048]{2,0,1:T(8,128)(2,1)S(1)}, bf16[176,2,2048]{2,0,1:T(8,128)(2,1)}, u32[]{:S(2)}) copy-start(bf16[176,2,2048]{2,0,1:T(8,128)(2,1)} %copy-done) | copy-start | bytes 4325380
  465.2 5.1 %copy-start.2 = (bf16[512,2048]{1,0:T(8,128)(2,1)S(1)}, bf16[512,2048]{1,0:T(8,128)(2,1)}, u32[]{:S(2)}) copy-start(bf16[512,2048]{1,0:T(8,128)(2,1)} %all-gather.4.cloned.1.call-done) | copy-start | bytes 6291460
Sparse Core Ops, SparseCore 0:
  147.2 50.8 all-gather.3
  363.1 45.3 reduce-scatter.1
where the time goes:
time: 480 us; the launch traced here: 479 us
  waiting for transfers between devices  176 us (37%)
  blocking collectives  140 us (29%)
  local copies, waits for them, and re-layouts  72.6 us (15%)
  other arithmetic  36.2 us (8%)
  starting transfers between devices  30.4 us (6%)
  between operations  14.3 us (3%)
  matrix products  8.77 us (2%)
    all_to_all x1, waiting for transfers between devices, body(): lax.all_to_all(outgoing, 'dp', split_axis=2, concat_axis=2, tiled=True)  123 us
    all_gather x1, blocking collectives, body(): lax.all_gather(merge_weights, 'dp', axis=0, tiled=True)  53.9 us
    all_gather x1, waiting for transfers between devices, body(): full_cot = lax.all_gather(cotangent, 'tensor', axis=1, tiled=True)  53 us
    all_gather x1, blocking collectives, body(): lax.all_gather(expert_ids, 'dp', axis=0, tiled=True)  50.6 us
    all_to_all x1, blocking collectives, body(): lax.all_to_all(slotted.astype(jnp.bfloat16), 'dp', split_axis=1, concat_a...  35.5 us
    select_n x1, local copies, waits for them, and re-layouts, body(): jnp.take(by_expert, pools_all.T, axis=1).reshape(ff_local, POOL, width)  22.3 us
    unnamed x20, local copies, waits for them, and re-layouts  17.2 us
    gather x1, local copies, waits for them, and re-layouts, body(): jnp.take(by_expert, pools_all.T, axis=1).reshape(ff_local, POOL, width)  13.3 us
  transfers between devices with their start and end apart: 5, of which 2 were waited for; matrix products, arithmetic and copies ran while one was open for 11% of the time, Pallas kernels for 0%

commit v1 on v0

--- a/solution.py
+++ b/solution.py
@@ -6,6 +6,20 @@
 E = 32
 K = 4
 POOL = 6
+
+
+def _follow_classes(ax_name, work_x):
+    dev_n = lax.psum(1, ax_name)
+    h_now = sorted(((i, (i + 1) % dev_n) for i in range(dev_n)))
+    val = work_x
+    block_list = [val]
+    for k0 in range(1, dev_n):
+        val = lax.ppermute(val, ax_name, h_now)
+        block_list.insert(0, val)
+    a_now = jnp.concatenate(block_list, axis=1)
+    lower = lax.axis_index(ax_name) + 1
+    local_now = jnp.roll(a_now, lower * work_x.shape[1], axis=1)
+    return local_now
 
 
 def pool_members(id_rows):
@@ -55,7 +69,7 @@
     layer_out = lax.psum_scatter(
         partial_rows.astype(jnp.bfloat16), "tensor", scatter_dimension=1, tiled=True
     )
-    full_cot = lax.all_gather(cotangent, "tensor", axis=1, tiled=True)
+    full_cot = _follow_classes("tensor", cotangent)
     cot_seg = full_cot.reshape(seg_count, seg_len, width)
     grad_hidden = (
         jnp.einsum("std,fsd->stf", cot_seg, merged, preferred_element_type=jnp.float32)

time: 480 us -> 478 us (level)
  waiting for transfers between devices: 176 us -> 160 us
  starting transfers between devices: 30.4 us -> 45.8 us
    ppermute x0 -> x7, waiting for transfers between devices: none -> 55.2 us  [_follow_classes(): val = lax.ppermute(val, ax_name, h_now)]
    all_gather x1 -> x0, waiting for transfers between devices: 53 us -> none  [body(): full_cot = lax.all_gather(cotangent, 'tensor', axis=1, tiled=True)]
    all_to_all x1, waiting for transfers between devices: 123 us -> 105 us  [body(): lax.all_to_all(outgoing, 'dp', split_axis=2, concat_axis=2, tiled=True)]
    ppermute x0 -> x7, starting transfers between devices: none -> 15.5 us  [_follow_classes(): val = lax.ppermute(val, ax_name, h_now)]
    unnamed x20 -> x37, local copies, waits for them, and re-layouts: 17.2 us -> 17 us
  transfers between devices with their start and end apart: 5 -> 11, of which waited for: 2 -> 8; matrix products, arithmetic and copies ran while one was open for 11% -> 10% of each run, Pallas kernels for 0% -> 0%
where the time goes in v1:
time: 478 us; the launch traced here: 477 us
  waiting for transfers between devices  160 us (33%)
  blocking collectives  140 us (29%)
  local copies, waits for them, and re-layouts  72.6 us (15%)
  starting transfers between devices  45.8 us (10%)
  other arithmetic  34.9 us (7%)
  between operations  14.6 us (3%)
  matrix products  8.77 us (2%)
    all_to_all x1, waiting for transfers between devices, body(): lax.all_to_all(outgoing, 'dp', split_axis=2, concat_axis=2, tiled=True)  105 us
    ppermute x7, waiting for transfers between devices, _follow_classes(): val = lax.ppermute(val, ax_name, h_now)  55.2 us
    all_gather x1, blocking collectives, body(): lax.all_gather(merge_weights, 'dp', axis=0, tiled=True)  53.9 us
    all_gather x1, blocking collectives, body(): lax.all_gather(expert_ids, 'dp', axis=0, tiled=True)  50.6 us
    all_to_all x1, blocking collectives, body(): lax.all_to_all(slotted.astype(jnp.bfloat16), 'dp', split_axis=1, concat_a...  35.7 us
    select_n x1, local copies, waits for them, and re-layouts, body(): jnp.take(by_expert, pools_all.T, axis=1).reshape(ff_local, POOL, width)  22.3 us
    unnamed x37, local copies, waits for them, and re-layouts  17 us
    ppermute x7, starting transfers between devices, _follow_classes(): val = lax.ppermute(val, ax_name, h_now)  15.5 us
  transfers between devices with their start and end apart: 11, of which 8 were waited for; matrix products, arithmetic and copies ran while one was open for 10% of the time, Pallas kernels for 0%

profile of v1, /device:TPU:1, one launch (start us, length us, event | category | flops | bytes accessed | tf_op | source)
XLA Modules:
  0.0 477.1 jit_solution(12074160636776424067)
XLA Ops:
  7.2 4.5 copy.81
  12.3 11.6 %reduce.2 = bf16[2048,176]{1,0:T(8,128)(2,1)S(1)} reduce(bf16[2048,1,176]{2,1,0:T(2,128)(2,1)S(1)} %bitcast.54, bf16[]{:T(256)} %broadcast.43), dimensions={1}, to_apply=%bitcast.43.reduce_sub_computation | reduce | bytes 1441794
  26.5 11.6 %all-to-all-start = ((bf16[64,2,2816]{2,1,0:T(2,128)(2,1)}), bf16[64,2,2816]{2,1,0:T(2,128)(2,1)S(1)}, u32[]{:S(2)}, u32[]{:S(2)}) async-start(bf16[64,2,2816]{2,1,0:T(2,128)(2,1)} %reshape.124), calls=%async_computation | async-start | bytes 1441792 | tf_op jit(solution)/shard_map/all_to_all | solution.py:58
  38.1 50.6 %all-gather = s32[64,2,4]{2,1,0:T(2,128)S(1)} all-gather(s32[1,2,4]{2,1,0:T(2,128)S(1)} %bitcast.64), channel_id=1, replica_groups=mesh['dp'=64,'tensor'=8] {'dp'}, dimensions={0}, use_global_device_ids=true | all-gather | bytes 2080 | tf_op jit(solution)/shard_map/all_gather | solution.py:49
  93.9 13.3 %gather_fusion.1 = bf16[384,176,32]{1,2,0:T(8,128)(2,1)} fusion(bf16[176,32,32]{0,2,1:T(8,128)(2,1)S(1)} %select_bitcast_fusion, s32[1024]{0:T(1024)S(1)} %pad_clamp_fusion), kind=kCustom, calls=%fused_computation.1 | custom fusion | bytes 8652288 | tf_op jit(solution)/shard_map/jit(_take)/gather | solution.py:60
  107.2 6.2 %broadcast_select_fusion = bf16[176,6,2048]{0,2,1:T(8,128)(2,1)S(1)} fusion(bf16[176,6,2048]{0,2,1:T(8,128)(2,1)} %bitcast.50, pred[6,2048]{1,0:T(8,128)(4,1)S(1)} %broadcast_in_dim.86), kind=kLoop, calls=%fused_computation.7 | loop fusion | flops 2162688 | bytes 8663040 | tf_op jit(solution)/shard_map/jit(_take)/select_n | solution.py:60
  113.4 22.3 %copy.82 = bf16[176,6,2048]{0,1,2:T(8,128)(2,1)} copy(bf16[176,6,2048]{0,2,1:T(8,128)(2,1)S(1)} %broadcast_select_fusion) | data formatting | bytes 8650752 | tf_op jit(solution)/shard_map/jit(_take)/select_n | solution.py:60
  135.7 8.6 %all-to-all-start.1 = ((bf16[176,6,2048]{0,1,2:T(8,128)(2,1)}), bf16[176,6,2048]{0,1,2:T(8,128)(2,1)}, u32[]{:S(2)}, u32[]{:S(2)}) async-start(bf16[176,6,2048]{0,1,2:T(8,128)(2,1)} %copy.82), calls=%async_computation.1 | async-start | bytes 16777216 | tf_op jit(solution)/shard_map/all_to_all | solution.py:61
  144.3 4.0 collective-permute-start
  148.3 13.0 %collective-permute-done = bf16[512,256]{1,0:T(8,128)(2,1)S(1)} collective-permute-done((bf16[512,256]{1,0:T(8,128)(2,1)S(1)}, bf16[512,256]{1,0:T(8,128)(2,1)S(1)}, u32[]{:S(2)}, u32[]{:S(2)}) %collective-permute-start) | collective-permute-done | bytes 262176 | tf_op jit(solution)/shard_map/ppermute | solution.py:17
  163.2 8.1 %collective-permute-done.1 = bf16[512,256]{1,0:T(8,128)(2,1)S(1)} collective-permute-done((bf16[512,256]{1,0:T(8,128)(2,1)S(1)}, bf16[512,256]{1,0:T(8,128)(2,1)S(1)}, u32[]{:S(2)}, u32[]{:S(2)}) %collective-permute-start.1) | collective-permute-done | bytes 262176 | tf_op jit(solution)/shard_map/ppermute | solution.py:17
  173.3 7.3 %collective-permute-done.2 = bf16[512,256]{1,0:T(8,128)(2,1)S(1)} collective-permute-done((bf16[512,256]{1,0:T(8,128)(2,1)S(1)}, bf16[512,256]{1,0:T(8,128)(2,1)S(1)}, u32[]{:S(2)}, u32[]{:S(2)}) %collective-permute-start.2) | collective-permute-done | bytes 262176 | tf_op jit(solution)/shard_map/ppermute | solution.py:17
  182.5 6.8 %collective-permute-done.3 = bf16[512,256]{1,0:T(8,128)(2,1)S(1)} collective-permute-done((bf16[512,256]{1,0:T(8,128)(2,1)S(1)}, bf16[512,256]{1,0:T(8,128)(2,1)S(1)}, u32[]{:S(2)}, u32[]{:S(2)}) %collective-permute-start.3) | collective-permute-done | bytes 262176 | tf_op jit(solution)/shard_map/ppermute | solution.py:17
  191.2 6.8 %collective-permute-done.4 = bf16[512,256]{1,0:T(8,128)(2,1)S(1)} collective-permute-done((bf16[512,256]{1,0:T(8,128)(2,1)S(1)}, bf16[512,256]{1,0:T(8,128)(2,1)S(1)}, u32[]{:S(2)}, u32[]{:S(2)}) %collective-permute-start.4) | collective-permute-done | bytes 262176 | tf_op jit(solution)/shard_map/ppermute | solution.py:17
  199.9 6.8 %collective-permute-done.5 = bf16[512,256]{1,0:T(8,128)(2,1)S(1)} collective-permute-done((bf16[512,256]{1,0:T(8,128)(2,1)S(1)}, bf16[512,256]{1,0:T(8,128)(2,1)S(1)}, u32[]{:S(2)}, u32[]{:S(2)}) %collective-permute-start.5) | collective-permute-done | bytes 262176 | tf_op jit(solution)/shard_map/ppermute | solution.py:17
  208.7 6.4 %collective-permute-done.6 = bf16[512,256]{1,0:T(8,128)(2,1)S(1)} collective-permute-done((bf16[512,256]{1,0:T(8,128)(2,1)S(1)}, bf16[512,256]{1,0:T(8,128)(2,1)S(1)}, u32[]{:S(2)}, u32[]{:S(2)}) %collective-permute-start.6) | collective-permute-done | bytes 262176 | tf_op jit(solution)/shard_map/ppermute | solution.py:17
  221.6 105.1 %all-to-all-done.1 = bf16[176,6,2048]{0,1,2:T(8,128)(2,1)} async-done(((bf16[176,6,2048]{0,1,2:T(8,128)(2,1)}), bf16[176,6,2048]{0,1,2:T(8,128)(2,1)}, u32[]{:S(2)}, u32[]{:S(2)}) %all-to-all-start.1) | async-done | bytes 4325408 | tf_op jit(solution)/shard_map/all_to_all | solution.py:61
  326.7 10.1 %all-to-all-start.2 = ((bf16[176,2,2048]{0,1,2:T(2,128)(2,1)}), bf16[176,2,2048]{0,1,2:T(2,128)(2,1)S(1)}, u32[]{:S(2)}, u32[]{:S(2)}) async-start(bf16[176,2,2048]{0,1,2:T(2,128)(2,1)} %copy.87), calls=%async_computation.3 | async-start | bytes 4194304 | tf_op jit(solution)/shard_map/all_to_all | solution.py:82
  337.1 11.3 %copy.83 = bf16[176,6,2048]{2,0,1:T(8,128)(2,1)} copy(bf16[176,6,2048]{0,1,2:T(8,128)(2,1)} %all-to-all-done.1) | data formatting | bytes 8650752 | tf_op jit(solution)/shard_map/all_to_all | solution.py:61
  348.4 6.6 %convert_element_type.65 = f32[176,6,2048]{2,0,1:T(8,128)} convert(bf16[176,6,2048]{2,0,1:T(8,128)(2,1)} %copy.83) | non-fusion elementwise | flops 2162688 | bytes 12976128 | tf_op jit(solution)/shard_map/convert_element_type | solution.py:63
  355.0 4.8 multiply_reduce_fusion.1
  363.0 53.9 %all-gather.1 = f32[64,2,4]{2,1,0:T(2,128)S(1)} all-gather(f32[1,2,4]{2,1,0:T(2,128)S(1)} %bitcast.65), channel_id=1, replica_groups=mesh['dp'=64,'tensor'=8] {'dp'}, dimensions={0}, use_global_device_ids=true | all-gather | bytes 2080 | tf_op jit(solution)/shard_map/all_gather | solution.py:50
  417.7 4.2 multiply_reduce_fusion
  428.2 35.7 %all_to_all.31 = bf16[176,64,32]{0,2,1:T(8,128)(2,1)S(1)} all-to-all(bf16[176,64,32]{0,2,1:T(8,128)(2,1)S(1)} %convert_element_type.76), channel_id=1, replica_groups=mesh['dp'=64,'tensor'=8] {'dp'}, dimensions={1} | all-to-all | bytes 1441792 | tf_op jit(solution)/shard_map/all_to_all | solution.py:98
  (84 shorter events, 43.0 us)
Async XLA Ops:
  7.2 31.0 %copy-start.5 = (s32[2,4]{1,0:T(2,128)S(1)}, s32[2,4]{1,0:T(2,128)}, u32[]{:S(2)}) copy-start(s32[2,4]{1,0:T(2,128)} %param.9) | copy-start | bytes 100
  7.2 82.5 %copy-start.7 = (s32[32]{0:T(128)S(1)}, s32[32]{0:T(128)}, u32[]{:S(2)}) copy-start(s32[32]{0:T(128)} %param.11) | copy-start | bytes 388
  26.5 63.3 %all-to-all-start = ((bf16[64,2,2816]{2,1,0:T(2,128)(2,1)}), bf16[64,2,2816]{2,1,0:T(2,128)(2,1)S(1)}, u32[]{:S(2)}, u32[]{:S(2)}) async-start(bf16[64,2,2816]{2,1,0:T(2,128)(2,1)} %reshape.124), calls=%async_computation | async-start | bytes 1441792 | tf_op jit(solution)/shard_map/all_to_all | solution.py:58
  135.7 8.6 %copy-start.3 = (bf16[512,256]{1,0:T(8,128)(2,1)S(1)}, bf16[512,256]{1,0:T(8,128)(2,1)}, u32[]{:S(2)}) copy-start(bf16[512,256]{1,0:T(8,128)(2,1)} %param.7) | copy-start | bytes 786436
  135.7 191.0 %all-to-all-start.1 = ((bf16[176,6,2048]{0,1,2:T(8,128)(2,1)}), bf16[176,6,2048]{0,1,2:T(8,128)(2,1)}, u32[]{:S(2)}, u32[]{:S(2)}) async-start(bf16[176,6,2048]{0,1,2:T(8,128)(2,1)} %copy.82), calls=%async_computation.1 | async-start | bytes 16777216 | tf_op jit(solution)/shard_map/all_to_all | solution.py:61
  144.3 17.0 %collective-permute-start = (bf16[512,256]{1,0:T(8,128)(2,1)S(1)}, bf16[512,256]{1,0:T(8,128)(2,1)S(1)}, u32[]{:S(2)}, u32[]{:S(2)}) collective-permute-start(bf16[512,256]{1,0:T(8,128)(2,1)S(1)} %copy-done.3), channel_id=1, source_target_pairs={{0,1},{1,2},{2,3},{3,4},{4,5},{5,6},{6,7},{7,0},{8,9},{9,10},{10,1... | collective-permute-start | bytes 786440 | tf_op jit(solution)/shard_map/ppermute | solution.py:17
  161.3 10.0 %collective-permute-start.1 = (bf16[512,256]{1,0:T(8,128)(2,1)S(1)}, bf16[512,256]{1,0:T(8,128)(2,1)S(1)}, u32[]{:S(2)}, u32[]{:S(2)}) collective-permute-start(bf16[512,256]{1,0:T(8,128)(2,1)S(1)} %collective-permute-done), channel_id=1, source_target_pairs={{0,1},{1,2},{2,3},{3,4},{4,5},{5,6},{6,7},{7,0},{8,9},{9,10},{10,1... | collective-permute-start | bytes 786440 | tf_op jit(solution)/shard_map/ppermute | solution.py:17
  171.3 9.2 %collective-permute-start.2 = (bf16[512,256]{1,0:T(8,128)(2,1)S(1)}, bf16[512,256]{1,0:T(8,128)(2,1)S(1)}, u32[]{:S(2)}, u32[]{:S(2)}) collective-permute-start(bf16[512,256]{1,0:T(8,128)(2,1)S(1)} %collective-permute-done.1), channel_id=1, source_target_pairs={{0,1},{1,2},{2,3},{3,4},{4,5},{5,6},{6,7},{7,0},{8,9},{9,10},{10,1... | collective-permute-start | bytes 786440 | tf_op jit(solution)/shard_map/ppermute | solution.py:17
  180.6 8.7 %collective-permute-start.3 = (bf16[512,256]{1,0:T(8,128)(2,1)S(1)}, bf16[512,256]{1,0:T(8,128)(2,1)S(1)}, u32[]{:S(2)}, u32[]{:S(2)}) collective-permute-start(bf16[512,256]{1,0:T(8,128)(2,1)S(1)} %collective-permute-done.2), channel_id=1, source_target_pairs={{0,1},{1,2},{2,3},{3,4},{4,5},{5,6},{6,7},{7,0},{8,9},{9,10},{10,1... | collective-permute-start | bytes 786440 | tf_op jit(solution)/shard_map/ppermute | solution.py:17
  189.3 8.7 %collective-permute-start.4 = (bf16[512,256]{1,0:T(8,128)(2,1)S(1)}, bf16[512,256]{1,0:T(8,128)(2,1)S(1)}, u32[]{:S(2)}, u32[]{:S(2)}) collective-permute-start(bf16[512,256]{1,0:T(8,128)(2,1)S(1)} %collective-permute-done.3), channel_id=1, source_target_pairs={{0,1},{1,2},{2,3},{3,4},{4,5},{5,6},{6,7},{7,0},{8,9},{9,10},{10,1... | collective-permute-start | bytes 786440 | tf_op jit(solution)/shard_map/ppermute | solution.py:17
  198.0 8.7 %collective-permute-start.5 = (bf16[512,256]{1,0:T(8,128)(2,1)S(1)}, bf16[512,256]{1,0:T(8,128)(2,1)S(1)}, u32[]{:S(2)}, u32[]{:S(2)}) collective-permute-start(bf16[512,256]{1,0:T(8,128)(2,1)S(1)} %collective-permute-done.4), channel_id=1, source_target_pairs={{0,1},{1,2},{2,3},{3,4},{4,5},{5,6},{6,7},{7,0},{8,9},{9,10},{10,1... | collective-permute-start | bytes 786440 | tf_op jit(solution)/shard_map/ppermute | solution.py:17
  206.7 8.3 %collective-permute-start.6 = (bf16[512,256]{1,0:T(8,128)(2,1)S(1)}, bf16[512,256]{1,0:T(8,128)(2,1)S(1)}, u32[]{:S(2)}, u32[]{:S(2)}) collective-permute-start(bf16[512,256]{1,0:T(8,128)(2,1)S(1)} %collective-permute-done.5), channel_id=1, source_target_pairs={{0,1},{1,2},{2,3},{3,4},{4,5},{5,6},{6,7},{7,0},{8,9},{9,10},{10,1... | collective-permute-start | bytes 786440 | tf_op jit(solution)/shard_map/ppermute | solution.py:17
  215.3 1.9 copy-start.4
  215.9 1.4 copy-start
  217.8 119.2 %copy-start.6 = (f32[2,4]{1,0:T(2,128)S(1)}, f32[2,4]{1,0:T(2,128)}, u32[]{:S(2)}) copy-start(f32[2,4]{1,0:T(2,128)} %param.10) | copy-start | bytes 100
  326.7 90.3 %all-to-all-start.2 = ((bf16[176,2,2048]{0,1,2:T(2,128)(2,1)}), bf16[176,2,2048]{0,1,2:T(2,128)(2,1)S(1)}, u32[]{:S(2)}, u32[]{:S(2)}) async-start(bf16[176,2,2048]{0,1,2:T(2,128)(2,1)} %copy.87), calls=%async_computation.3 | async-start | bytes 4194304 | tf_op jit(solution)/shard_map/all_to_all | solution.py:82
  336.8 133.5 %reduce-scatter.2.cloned.1.call-start = ((), (), s32[]{:S(2)}) async-start(), calls=%async_computation.5 | async-start | bytes 2359296 | tf_op jit(solution)/shard_map/reduce_scatter | solution.py:69
  359.8 1.1 copy-start.1
  428.2 38.9 %copy-start.2 = (bf16[176,2,2048]{2,0,1:T(8,128)(2,1)S(1)}, bf16[176,2,2048]{2,0,1:T(8,128)(2,1)}, u32[]{:S(2)}) copy-start(bf16[176,2,2048]{2,0,1:T(8,128)(2,1)} %copy-done.1) | copy-start | bytes 4325380
Sparse Core Ops, SparseCore 0:
  363.1 45.3 reduce-scatter.1
